TPU v7x, 32 devices: a whole 2x2x4 slice. The times are simulated.
32 devices in a mesh: dp: 4 (over y, x), seq: 8 (over z, core).
Axes of the slice: x: 2, y: 2, z: 4, core: 2. Of those that a mesh axis runs over, the one named last changes fastest.
Arguments:
- student_x: bfloat16 [4096, 4096], P(('dp', 'seq')), parts along dimension 0, may hold values from -60 to 60
- student_z: bfloat16 [4096, 4096], P(('dp', 'seq')), parts along dimension 0, may hold values from -6 to 6
- student_b: bfloat16 [4096, 1024], P(('dp', 'seq')), parts along dimension 0, may hold values from -0.5 to 0.5
- student_c: bfloat16 [4096, 1024], P(('dp', 'seq')), parts along dimension 0, may hold values from -6 to 6
- step_size: float32 [64, 4096], P(None, ('dp', 'seq')), parts along dimension 1, may hold values from 0 to 1
- decay_rate: float32 [64], replicated, may hold values from 0.5 to 2
- norm_gain: float32 [4096], replicated, may hold values from 0.5 to 1.5
- teacher_q: bfloat16 [4096, 4096], P(('dp', 'seq')), parts along dimension 0, may hold values from -140 to 140
- teacher_k: bfloat16 [4096, 1024], P(('dp', 'seq')), parts along dimension 0, may hold values from -7 to 7
- teacher_v: bfloat16 [4096, 1024], P(('dp', 'seq')), parts along dimension 0, may hold values from -6 to 6
Outputs:
- student_out: bfloat16 [4096, 4096], P(('dp', 'seq')), parts along dimension 0
- teacher_out: bfloat16 [4096, 4096], P(('dp', 'seq')), parts along dimension 0
There are 4 independent parts, one for each index of `dp`. A program takes and returns all parts, laid end to end along the dimension named above; an argument that names none is the same for every part. Nothing has to cross between parts.
All inputs are finite; a program needn't handle non-finite values.
Results may differ from a plain program's by a relative error of at most 0.0075.
Values may be sent and summed in bfloat16 or wider, within the bound.
A program may use at most 256 MiB of HBM per device.

v0:
```python
import math
import jax
import jax.numpy as jnp
from jax import lax
from jax.sharding import PartitionSpec as P

GROUPS = 8
HEAD_SIZE = 128
BLOCK = 128
epsilon_norm = 1e-05
masked_score = -1e30
HIGHEST = lax.Precision.HIGHEST


def entering(array, axis, combine, identity):
    devices, place = (lax.axis_size(axis), lax.axis_index(axis))
    everything = jax.tree.map(
        lambda part, kind: lax.all_gather(part.astype(kind), axis),
        array,
        (jnp.bfloat16, jnp.bfloat16),
    )
    start = jax.tree.map(
        lambda part, zero: jnp.broadcast_to(jnp.asarray(zero, part.dtype), part.shape),
        array,
        identity,
    )

    def step(k, before):
        reached = k < place
        new = combine(
            before, jax.tree.map(lambda part, own: part[k].astype(own.dtype), everything, array)
        )
        return jax.tree.map(lambda a, b: jnp.where(reached, a, b), new, before)

    return lax.fori_loop(0, devices, step, start)


def block_pass(carry_state, block_inputs, decay_rate, group_count):
    x_block, b_block, c_block, step_block = block_inputs
    block_rows = x_block.shape[0]
    head_count = step_block.shape[0]
    state_dim = b_block.shape[1] // group_count
    per_group = head_count // group_count
    head_width = x_block.shape[1] // head_count
    log_decay = -step_block * decay_rate[:, None]
    running = jnp.cumsum(log_decay, axis=1)
    b_three = b_block.reshape(block_rows, group_count, state_dim)
    c_three = c_block.reshape(block_rows, group_count, state_dim)
    x_four = x_block.reshape(block_rows, group_count, per_group, head_width)
    products = jnp.einsum("tgn,sgn->gts", c_three, b_three, preferred_element_type=jnp.float32)
    lower_mask = jnp.arange(block_rows)[:, None] >= jnp.arange(block_rows)[None, :]
    spread = running[:, :, None] - running[:, None, :]
    factor = jnp.exp(jnp.where(lower_mask[None], spread, masked_score))
    weights = (
        products[:, None] * factor.reshape(group_count, per_group, block_rows, block_rows)
    ).astype(jnp.bfloat16)
    local_out = jnp.einsum("gkts,sgkp->tgkp", weights, x_four, preferred_element_type=jnp.float32)
    state_four = carry_state.reshape(group_count, per_group, head_width, state_dim)
    carried = jnp.einsum(
        "tgn,gkpn->tgkp", c_three.astype(jnp.float32), state_four, precision=HIGHEST
    )
    carried = carried * jnp.exp(running).T.reshape(block_rows, group_count, per_group, 1)
    tail_decay = jnp.exp(running[:, -1:] - running)
    scaled = x_four.astype(jnp.float32) * tail_decay.T.reshape(
        block_rows, group_count, per_group, 1
    )
    fresh_state = jnp.einsum(
        "sgkp,sgn->gkpn", scaled, b_three.astype(jnp.float32), precision=HIGHEST
    )
    new_state = (
        jnp.exp(running[:, -1]).reshape(group_count, per_group, 1, 1) * state_four + fresh_state
    )
    combined = (local_out + carried).reshape(block_rows, head_count * head_width)
    return (new_state.reshape(head_count, head_width, state_dim), combined)


def attend_block(fold_carry, query_four, key_block, value_block, key_start, query_pos, score_scale):
    row_max, row_total, weighted = fold_carry
    key_rows = key_block.shape[0]
    kv_count = query_four.shape[1]
    head_width = query_four.shape[3]
    keys_three = key_block.reshape(key_rows, kv_count, head_width)
    values_three = value_block.reshape(key_rows, kv_count, head_width)
    scores = (
        jnp.einsum("qgkd,sgd->qgks", query_four, keys_three, preferred_element_type=jnp.float32)
        * score_scale
    )
    key_pos = key_start + jnp.arange(key_rows)
    visible = (key_pos[None, :] <= query_pos[:, None])[:, None, None, :]
    masked = jnp.where(visible, scores, masked_score)
    new_max = jnp.maximum(row_max, jnp.max(masked, axis=3))
    shrink = jnp.exp(row_max - new_max)
    probabilities = jnp.where(visible, jnp.exp(masked - new_max[..., None]), 0.0)
    row_total = row_total * shrink + jnp.sum(probabilities, axis=3)
    update = jnp.einsum(
        "qgks,sgd->qgkd",
        probabilities.astype(jnp.bfloat16),
        values_three,
        preferred_element_type=jnp.float32,
    )
    weighted = weighted * shrink[..., None] + update
    return (new_max, row_total, weighted)


def on_device(
    student_x,
    student_z,
    student_b,
    student_c,
    step_size,
    decay_rate,
    norm_gain,
    teacher_q,
    teacher_k,
    teacher_v,
):
    tokens, width = student_x.shape
    head_count = step_size.shape[0]
    head_width = width // head_count
    group_count = GROUPS
    per_group = head_count // group_count
    state_dim = student_b.shape[1] // group_count
    block_count = tokens // BLOCK
    my_index = lax.axis_index("seq")
    blocks_in = (
        student_x.reshape(block_count, BLOCK, width),
        student_b.reshape(block_count, BLOCK, group_count * state_dim),
        student_c.reshape(block_count, BLOCK, group_count * state_dim),
        step_size.reshape(head_count, block_count, BLOCK).transpose(1, 0, 2),
    )

    def advance(carry_state, block_inputs):
        return block_pass(carry_state, block_inputs, decay_rate, group_count)

    zero_state = jnp.zeros((head_count, head_width, state_dim), jnp.float32)
    local_state, block_outs = lax.scan(advance, zero_state, blocks_in)
    cum_device = jnp.cumsum(-step_size * decay_rate[:, None], axis=1)
    device_decay = jnp.exp(cum_device[:, -1])

    def combine(earlier, following):
        return (earlier[0] * following[0], following[0][:, None, None] * earlier[1] + following[1])

    identity = (jnp.ones_like(device_decay), jnp.zeros_like(local_state))
    incoming = entering((device_decay, local_state), "seq", combine, identity)[1]
    ratio = teacher_q.shape[1] // teacher_k.shape[1]
    kv_count = teacher_k.shape[1] // HEAD_SIZE
    query_four = teacher_q.reshape(tokens, kv_count, ratio, HEAD_SIZE)
    query_pos = my_index * tokens + jnp.arange(tokens)
    score_scale = 1.0 / math.sqrt(HEAD_SIZE)
    start_carry = (
        jnp.full((tokens, kv_count, ratio), masked_score, jnp.float32),
        jnp.zeros((tokens, kv_count, ratio), jnp.float32),
        jnp.zeros((tokens, kv_count, ratio, HEAD_SIZE), jnp.float32),
    )
    key_piece = lax.all_gather(teacher_k, "seq", axis=0, tiled=True)
    value_piece = lax.all_gather(teacher_v, "seq", axis=0, tiled=True)
    piece_rows = key_piece.shape[0]
    sub_rows = math.gcd(piece_rows, 512)

    def visit_block(block_index, current):
        key_block = lax.dynamic_slice_in_dim(key_piece, block_index * sub_rows, sub_rows, 0)
        value_block = lax.dynamic_slice_in_dim(value_piece, block_index * sub_rows, sub_rows, 0)
        return attend_block(
            current,
            query_four,
            key_block,
            value_block,
            block_index * sub_rows,
            query_pos,
            score_scale,
        )

    final_carry = lax.fori_loop(0, piece_rows // sub_rows, visit_block, start_carry)
    _, row_total, weighted = final_carry
    teacher_out = (
        (weighted / row_total[..., None])
        .reshape(tokens, kv_count * ratio * HEAD_SIZE)
        .astype(jnp.bfloat16)
    )
    c_three = student_c.reshape(tokens, group_count, state_dim).astype(jnp.float32)
    in_four = incoming.reshape(group_count, per_group, head_width, state_dim)
    carried_in = jnp.einsum("tgn,gkpn->tgkp", c_three, in_four, precision=HIGHEST)
    carried_in = carried_in * jnp.exp(cum_device).T.reshape(tokens, group_count, per_group, 1)
    combined = block_outs.reshape(tokens, group_count, per_group, head_width) + carried_in
    gated_out = combined.reshape(tokens, head_count, head_width) * jax.nn.silu(
        student_z.astype(jnp.float32)
    ).reshape(tokens, head_count, head_width)
    mean_square = jnp.mean(gated_out * gated_out, axis=2, keepdims=True)
    normed = (
        gated_out
        * lax.rsqrt(mean_square + epsilon_norm)
        * norm_gain.reshape(1, head_count, head_width)
    )
    student_out = normed.reshape(tokens, width).astype(jnp.bfloat16)
    return (student_out, teacher_out)


def solution(mesh):
    return jax.shard_map(
        on_device,
        mesh=mesh,
        in_specs=(
            P(("dp", "seq"), None),
            P(("dp", "seq"), None),
            P(("dp", "seq"), None),
            P(("dp", "seq"), None),
            P(None, ("dp", "seq")),
            P(),
            P(),
            P(("dp", "seq"), None),
            P(("dp", "seq"), None),
            P(("dp", "seq"), None),
        ),
        out_specs=(P(("dp", "seq"), None), P(("dp", "seq"), None)),
        check_vma=False,
    )
```

profile of v0, /device:TPU:0, one launch (start us, length us, event | category | flops | bytes accessed | tf_op | source)
XLA Modules:
  0.0 190.1 jit_solution(6066163782654913500)
XLA Ops:
  7.2 1.9 copy.44
  9.2 1.8 copy.46
  13.3 2.2 %add_convert_fusion = bf16[8,8,64,128]{3,2,1,0:T(8,128)(2,1)} fusion(bf16[128,8,8,64]{0,3,2,1:T(8,128)(2,1)S(1)} %bitcast.130, f32[128,8,8]{0,2,1:T(8,128)S(1)} %get-tuple-element.366, f32[8,8]{1,0:T(8,128)S(1)} %mul.192, bf16[128,8,128,1]{2,1,0,3:T(8,128)(2,1)S(1)} %bitcast.135), kind=kOutput, calls=%fused_computation.42 | convolution fusion | flops 807403520 | bytes 2392320 | tf_op jit(solution)/shard_map/while/body/eval_jaxpr/sgkp,sgn->gkpn/dot_general | solution.py:67
  17.3 19.1 %all-reduce = bf16[512]{0:T(512)(128)(2,1)S(1)} all-reduce(bf16[512]{0:T(512)(128)(2,1)S(1)} %dynamic-update-slice), channel_id=2, replica_groups=mesh['dp'=4,'seq'=8] {'seq'}, use_global_device_ids=true, to_apply=%add | all-reduce | flops 512 | bytes 2048
  39.4 2.3 %copy.45 = bf16[128,4096]{0,1:T(8,128)(2,1)} copy(bf16[128,4096]{1,0:T(8,128)(2,1)} %param.21) | data formatting | bytes 2097152 | tf_op args[7]
  41.7 1.6 copy.47
  43.4 1.4 fusion.36
  44.8 2.3 %fusion.34 = f32[8,8,64,128]{3,2,1,0:T(8,128)} fusion(bf16[128,8,128,1]{2,1,0,3:T(8,128)(2,1)S(1)} %bitcast.127), kind=kOutput, calls=%fused_computation.52 | convolution fusion | flops 805306368 | bytes 2359296 | tf_op jit(solution)/shard_map/while/body/eval_jaxpr/tgn,gkpn->tgkp/dot_general | solution.py:59
  47.1 3.2 %fusion.18 = f32[8,8,128,64]{2,3,1,0:T(8,128)} fusion(bf16[128,8,8,64]{0,3,2,1:T(8,128)(2,1)S(1)} %bitcast.131, f32[8,8,128]{2,1,0:T(8,128)S(1)} %bitcast.134, f32[8,128,128]{2,1,0:T(8,128)S(1)} %fusion.36, pred[128,128]{1,0:T(8,128)(4,1)S(1)} %iota_compare_fusion), kind=kOutput, calls=%fused_computation.31 | convolution fusion | flops 138412032 | bytes 3719168 | tf_op jit(solution)/shard_map/while/body/eval_jaxpr/gkts,sgkp->tgkp/dot_general | solution.py:57
  50.4 24.1 %all-gather.9.cloned.1.call-done = bf16[1024,1024]{0,1:T(8,128)(2,1)} async-done(((bf16[128,1024]{0,1:T(8,128)(2,1)}), bf16[1024,1024]{0,1:T(8,128)(2,1)}) %all-gather.9.cloned.1.call-update) | async-done | bytes 2097168 | tf_op jit(solution)/shard_map/all_gather | solution.py:156
  74.5 37.5 %while.38 = (s32[]{:T(128)}, f32[128,8,4]{0,2,1:T(4,128)S(1)}, f32[128,8,4]{0,2,1:T(4,128)S(1)}, f32[128,8,4,128]{0,3,2,1:T(8,128)}, bf16[1024,1024]{0,1:T(8,128...) while((s32[]{:T(128)}, f32[128,8,4]{0,2,1:T(4,128)S(1)}, ...), condition=%wide.region_7.8_spmd.clone, body=%wide.region_4.7_spmd.clone.sunk | while | flops 1102664320 | bytes 70784216 | solution.py:173
  74.5 2.6 %constant_dynamic-slice_fusion.3 = (bf16[512,1024]{0,1:T(8,128)(2,1)}, bf16[512,1024]{0,1:T(8,128)(2,1)S(1)}) fusion(bf16[1024,1024]{0,1:T(8,128)(2,1)} %get-tuple-element.512, s32[]{:T(128)S(6)} %select_n.96, bf16[1024,1024]{0,1:T(8,128)(2,1)} %get-tuple-element.510), kind=kLoop, calls=%fused_computation.20.clone.1 | loop fusion | bytes 4194308 | tf_op jit(solution)/shard_map/while/body/eval_jaxpr/dynamic_slice | solution.py:162
  77.3 4.7 %fusion.68 = (f32[128,8,4]{0,2,1:T(4,128)S(1)}, f32[8,512,128,4]{2,1,3,0:T(8,128)}) fusion(pred[128,512]{0,1:T(8,128)(4,1)S(1)} %broadcast_compare_fusion.2, bf16[512,8,128,1]{0,2,3,1:T(8,128)(2,1)S(1)} %bitcast.122, bf16[128,8,4,128]{3,0,2,1:T(8,128)(2,1)S(1)} %get-tuple-element.511), kind=kOutput, calls=%fused_computation.6.clone.1 | convolution fusion | flops 543158272 | bytes 10567680 | tf_op jit(solution)/shard_map/while/body/eval_jaxpr/qgkd,sgd->qgks/dot_general | solution.py:85
  82.0 5.7 %fusion.69 = f32[128,8,4]{0,2,1:T(4,128)S(1)} fusion(f32[8,512,128,4]{2,1,3,0:T(8,128)} %get-tuple-element.457, f32[128,8,4]{0,2,1:T(4,128)S(1)} %select_maximum_fusion.2, pred[128,512]{0,1:T(8,128)(4,1)S(1)} %broadcast_compare_fusion.2), kind=kLoop, calls=%fused_computation.8.clone.1 | loop fusion | flops 10481664 | bytes 8486912 | tf_op jit(solution)/shard_map/while/body/eval_jaxpr/reduce_sum | solution.py:94
  88.9 4.6 %bitcast_add_fusion.2 = f32[128,8,4,128]{0,3,2,1:T(8,128)} fusion(f32[128,8,4,128]{0,3,2,1:T(8,128)} %get-tuple-element.497, bf16[512,8,128,1]{0,2,3,1:T(8,128)(2,1)} %bitcast.124, f32[8,512,128,4]{2,1,3,0:T(8,128)S(1)} %copy-done, f32[128,8,4]{0,2,1:T(4,128)S(1)} %select_maximum_fusion.2, pred[128,512]{0,1:T(8,128)(4,1)S(1)} %broadcast_compare_fusion.2, ...), kind=kOutput, calls=%fused_computation.11.clone.1 | convolution fusion | flops 548929536 | bytes 13729793 | tf_op jit(solution)/shard_map/while/body/eval_jaxpr/qgks,sgd->qgkd/dot_general | solution.py:95
  93.5 2.6 %constant_dynamic-slice_fusion.3 = (bf16[512,1024]{0,1:T(8,128)(2,1)}, bf16[512,1024]{0,1:T(8,128)(2,1)S(1)}) fusion(bf16[1024,1024]{0,1:T(8,128)(2,1)} %get-tuple-element.512, s32[]{:T(128)S(6)} %select_n.96, bf16[1024,1024]{0,1:T(8,128)(2,1)} %get-tuple-element.510), kind=kLoop, calls=%fused_computation.20.clone.1 | loop fusion | bytes 4194308 | tf_op jit(solution)/shard_map/while/body/eval_jaxpr/dynamic_slice | solution.py:162
  96.3 4.7 %fusion.68 = (f32[128,8,4]{0,2,1:T(4,128)S(1)}, f32[8,512,128,4]{2,1,3,0:T(8,128)}) fusion(pred[128,512]{0,1:T(8,128)(4,1)S(1)} %broadcast_compare_fusion.2, bf16[512,8,128,1]{0,2,3,1:T(8,128)(2,1)S(1)} %bitcast.122, bf16[128,8,4,128]{3,0,2,1:T(8,128)(2,1)S(1)} %get-tuple-element.511), kind=kOutput, calls=%fused_computation.6.clone.1 | convolution fusion | flops 543158272 | bytes 10567680 | tf_op jit(solution)/shard_map/while/body/eval_jaxpr/qgkd,sgd->qgks/dot_general | solution.py:85
  101.0 4.8 %fusion.69 = f32[128,8,4]{0,2,1:T(4,128)S(1)} fusion(f32[8,512,128,4]{2,1,3,0:T(8,128)} %get-tuple-element.457, f32[128,8,4]{0,2,1:T(4,128)S(1)} %select_maximum_fusion.2, pred[128,512]{0,1:T(8,128)(4,1)S(1)} %broadcast_compare_fusion.2), kind=kLoop, calls=%fused_computation.8.clone.1 | loop fusion | flops 10481664 | bytes 8486912 | tf_op jit(solution)/shard_map/while/body/eval_jaxpr/reduce_sum | solution.py:94
  107.0 5.0 %bitcast_add_fusion.2 = f32[128,8,4,128]{0,3,2,1:T(8,128)} fusion(f32[128,8,4,128]{0,3,2,1:T(8,128)} %get-tuple-element.497, bf16[512,8,128,1]{0,2,3,1:T(8,128)(2,1)} %bitcast.124, f32[8,512,128,4]{2,1,3,0:T(8,128)S(1)} %copy-done, f32[128,8,4]{0,2,1:T(4,128)S(1)} %select_maximum_fusion.2, pred[128,512]{0,1:T(8,128)(4,1)S(1)} %broadcast_compare_fusion.2, ...), kind=kOutput, calls=%fused_computation.11.clone.1 | convolution fusion | flops 548929536 | bytes 13729793 | tf_op jit(solution)/shard_map/while/body/eval_jaxpr/qgks,sgd->qgkd/dot_general | solution.py:95
  112.0 1.9 %divide_convert_fusion = bf16[128,8,4,128]{0,3,2,1:T(8,128)(2,1)S(1)} fusion(f32[128,8,4,128]{0,3,2,1:T(8,128)} %get-tuple-element.261, f32[128,8,4]{0,2,1:T(4,128)S(1)} %get-tuple-element.262), kind=kLoop, calls=%fused_computation.40 | loop fusion | flops 1048576 | bytes 3162112 | tf_op jit(solution)/shard_map/convert_element_type | solution.py:178
  113.9 1.3 copy.62
  115.3 41.9 %all-gather.5.cloned.1.call-done = bf16[8,64,64,128]{3,2,1,0:T(8,128)(2,1)} async-done(((bf16[1,64,64,128]{3,2,1,0:T(8,128)(2,1)}), bf16[8,64,64,128]{3,2,1,0:T(8,128)(2,1)}) %all-gather.5.cloned.1.call-update) | async-done | bytes 8388624 | tf_op jit(solution)/shard_map/all_gather | solution.py:18
  157.2 19.8 %while.37 = (s32[]{:T(128)}, f32[64,64,128]{2,1,0:T(8,128)S(1)}, s32[]{:T(128)}, bf16[8,64]{1,0:T(8,128)(2,1)}, bf16[8,64,64,128]{3,2,1,0:T(8,128)(2,1)}, /*index=5*/s32[]{:T(128)}, s32[]{:T(128)}) while((s32[]{:T(128)}, f32[64,64,128]{2,1,0:T(8,128)S(1)}, s32[]{:T(128)}, bf16[8,64]{1,0:T(8,128)(2,1)}, ...), condition=%wide.region_2.3_spmd.clone, body=%wide.region_1.2_spmd.clone.sunk | while | flops 2621508 | bytes 5243625 | solution.py:35
  157.9 1.8 fusion.63
  160.4 1.8 fusion.63
  162.9 1.8 fusion.63
  165.3 1.8 fusion.63
  167.8 1.8 fusion.63
  170.3 1.8 fusion.63
  172.7 1.8 fusion.63
  175.2 1.8 fusion.63
  177.0 4.3 %multiply_reduce_fusion = (f32[128,8,8]{0,2,1:T(8,128)S(1)}, f32[128,8,8,64]{0,3,2,1:T(8,128)S(1)}) fusion(bf16[128,4096]{0,1:T(8,128)(2,1)S(1)} %copy-done.1, f32[8,8,64,128]{3,2,1,0:T(8,128)S(1)} %bitcast.123, bf16[128,8,128,1]{2,1,0,3:T(8,128)(2,1)S(1)} %bitcast.128, f32[128,8,8]{0,2,1:T(8,128)S(1)} %get-tuple-element.365, ...), kind=kOutput, calls=%fused_computation.41 | convolution fusion | flops 811589632 | bytes 9764864 | tf_op jit(solution)/shard_map/tgn,gkpn->tgkp/dot_general | solution.py:182
  (69 shorter events, 17.0 us)
Async XLA Ops:
  7.2 5.3 %copy-start.2 = (bf16[128,4096]{1,0:T(8,128)(2,1)S(1)}, bf16[128,4096]{1,0:T(8,128)(2,1)}, u32[]{:S(2)}) copy-start(bf16[128,4096]{1,0:T(8,128)(2,1)} %param.14) | copy-start | bytes 3145732
  7.2 6.0 %copy-start.6 = (bf16[128,1024]{1,0:T(8,128)(2,1)S(1)}, bf16[128,1024]{1,0:T(8,128)(2,1)}, u32[]{:S(2)}) copy-start(bf16[128,1024]{1,0:T(8,128)(2,1)} %param.16) | copy-start | bytes 786436
  7.2 43.2 %all-gather.7.cloned.1.call-start = ((), (), s32[]{:S(2)}) async-start(), calls=%async_computation.1 | async-start | bytes 2359296 | tf_op jit(solution)/shard_map/all_gather | solution.py:155
  9.1 65.4 %all-gather.9.cloned.1.call-start = ((), (), s32[]{:S(2)}) async-start(), calls=%async_computation.2 | async-start | bytes 2359296 | tf_op jit(solution)/shard_map/all_gather | solution.py:156
  11.0 146.2 %all-gather.5.cloned.1.call-start = ((), (), s32[]{:S(2)}) async-start(), calls=%async_computation | async-start | bytes 9437184 | tf_op jit(solution)/shard_map/all_gather | solution.py:18
  13.1 2.5 %copy-start.4 = (bf16[128,4096]{0,1:T(8,128)(2,1)}, bf16[128,4096]{0,1:T(8,128)(2,1)S(1)}, u32[]{:S(2)}) copy-start(bf16[128,4096]{0,1:T(8,128)(2,1)S(1)} %copy.39) | copy-start | bytes 3145732
  13.1 2.5 %copy-start.8 = (u32[32]{0:T(128)S(1)}, u32[32]{0:T(128)}, u32[]{:S(2)}) copy-start(u32[32]{0:T(128)} %constant.120) | copy-start | bytes 388
  13.2 24.9 %copy-start.3 = (bf16[128,4096]{1,0:T(8,128)(2,1)S(1)}, bf16[128,4096]{1,0:T(8,128)(2,1)}, u32[]{:S(2)}) copy-start(bf16[128,4096]{1,0:T(8,128)(2,1)} %param.15) | copy-start | bytes 3145732
  43.4 3.8 %copy-start.5 = (bf16[128,4096]{0,1:T(8,128)(2,1)S(1)}, bf16[128,4096]{0,1:T(8,128)(2,1)}, u32[]{:S(2)}) copy-start(bf16[128,4096]{0,1:T(8,128)(2,1)} %copy-done.4) | copy-start | bytes 3145732
  82.0 6.9 %copy-start = (f32[8,512,128,4]{2,1,3,0:T(8,128)S(1)}, f32[8,512,128,4]{2,1,3,0:T(8,128)}, u32[]{:S(2)}) copy-start(f32[8,512,128,4]{2,1,3,0:T(8,128)} %get-tuple-element.457) | copy-start | bytes 25165828 | tf_op jit(solution)/shard_map/while
  101.0 6.0 %copy-start = (f32[8,512,128,4]{2,1,3,0:T(8,128)S(1)}, f32[8,512,128,4]{2,1,3,0:T(8,128)}, u32[]{:S(2)}) copy-start(f32[8,512,128,4]{2,1,3,0:T(8,128)} %get-tuple-element.457) | copy-start | bytes 25165828 | tf_op jit(solution)/shard_map/while
  157.2 19.8 %copy-start.1 = (bf16[128,4096]{0,1:T(8,128)(2,1)S(1)}, bf16[128,4096]{0,1:T(8,128)(2,1)}, u32[]{:S(2)}) copy-start(bf16[128,4096]{0,1:T(8,128)(2,1)} %copy.43) | copy-start | bytes 3145732
  177.0 4.3 %copy-start.7 = (f32[4096]{0:T(1024)S(1)}, f32[4096]{0:T(1024)}, u32[]{:S(2)}) copy-start(f32[4096]{0:T(1024)} %param.20) | copy-start | bytes 49156
Sparse Core Ops, SparseCore 0:
  9.6 33.5 all-gather.6
  44.8 29.6 all-gather.8
  76.1 81.0 all-gather.4
where the time goes:
time: 191 us; the launch traced here: 190 us
  waiting for transfers between devices  66.1 us (35%)
  other arithmetic  35 us (18%)
  matrix products  32.5 us (17%)
  local copies, waits for them, and re-layouts  22.5 us (12%)
  blocking collectives  19.1 us (10%)
  between operations  14.6 us (8%)
    all_gather x1, waiting for transfers between devices, entering(): lax.all_gather(part.astype(kind), axis)  41.9 us
    all_gather x1, waiting for transfers between devices, on_device(): value_piece = lax.all_gather(teacher_v, 'seq', axis=0, tiled=True)  24.1 us
    unnamed x1, blocking collectives  19.1 us
    select_n x8, other arithmetic, step(): return jax.tree.map(lambda a, b: jnp.where(reached, a, b), new, before)  14.1 us
    unnamed x28, local copies, waits for them, and re-layouts  12.8 us
    reduce_sum x2, other arithmetic, attend_block(): row_total = row_total * shrink + jnp.sum(probabilities, axis=3)  10.5 us
    dot_general x2, matrix products, attend_block(): jnp.einsum('qgks,sgd->qgkd', probabilities.astype(jnp.bfloat16), values_t...  9.59 us
    dot_general x2, matrix products, attend_block(): jnp.einsum('qgkd,sgd->qgks', query_four, keys_three, preferred_element_ty...  9.4 us
  transfers between devices with their start and end apart: 3, of which 2 were waited for; matrix products, arithmetic and copies ran while one was open for 31% of the time, Pallas kernels for 0%

commit v1 on v0

--- a/solution.py
+++ b/solution.py
@@ -1,3 +1,4 @@
+import functools
 import math
 import jax
 import jax.numpy as jnp
@@ -10,6 +11,23 @@
 epsilon_norm = 1e-05
 masked_score = -1e30
 HIGHEST = lax.Precision.HIGHEST
+
+
+def save_members_all(s0, row_dim):
+    nd = jax.lax.axis_size("seq")
+    value_now = sorted(((kk, (kk + 1) % nd) for kk in range(nd)))
+    spare = s0
+    shelf = [spare]
+    for m in range(1, nd):
+        spare = jax.lax.ppermute(spare, axis_name="seq", perm=value_now)
+        shelf.insert(0, spare)
+    b_next = jnp.concatenate(shelf, row_dim)
+    block_now = jax.lax.axis_index("seq")
+    long_array = block_now + 1
+    return jnp.roll(b_next, long_array * s0.shape[row_dim], row_dim)
+
+
+area_wrap = functools.partial(save_members_all, row_dim=0)
 
 
 def entering(array, axis, combine, identity):
@@ -153,7 +171,7 @@
         jnp.zeros((tokens, kv_count, ratio, HEAD_SIZE), jnp.float32),
     )
     key_piece = lax.all_gather(teacher_k, "seq", axis=0, tiled=True)
-    value_piece = lax.all_gather(teacher_v, "seq", axis=0, tiled=True)
+    value_piece = area_wrap(teacher_v)
     piece_rows = key_piece.shape[0]
     sub_rows = math.gcd(piece_rows, 512)
 

time: 191 us -> 189 us (0.990)
  the two profiles are of different devices: /device:TPU:0 before, /device:TPU:16 now
where the time goes in v1:
time: 189 us; the launch traced here: 188 us
  waiting for transfers between devices  61.1 us (32%)
  matrix products  33.1 us (18%)
  local copies, waits for them, and re-layouts  29.8 us (16%)
  other arithmetic  28.5 us (15%)
  blocking collectives  16.9 us (9%)
  between operations  15.2 us (8%)
  starting transfers between devices  3.15 us (2%)
    ppermute x7, waiting for transfers between devices, save_members_all(): spare = jax.lax.ppermute(spare, axis_name='seq', perm=value_now)  61.1 us
    unnamed x55, local copies, waits for them, and re-layouts  19.1 us
    unnamed x1, blocking collectives  16.9 us
    select_n x8, other arithmetic, step(): return jax.tree.map(lambda a, b: jnp.where(reached, a, b), new, before)  14.3 us
    dot_general x2, matrix products, attend_block(): jnp.einsum('qgks,sgd->qgkd', probabilities.astype(jnp.bfloat16), values_t...  9.56 us
    dot_general x2, matrix products, attend_block(): jnp.einsum('qgkd,sgd->qgks', query_four, keys_three, preferred_element_ty...  9.41 us
    reduce_sum x2, other arithmetic, attend_block(): row_total = row_total * shrink + jnp.sum(probabilities, axis=3)  9.4 us
    dynamic_slice x2, local copies, waits for them, and re-layouts, visit_block(): lax.dynamic_slice_in_dim(value_piece, block_index * sub_rows, sub_rows, 0)  5.29 us
  transfers between devices with their start and end apart: 9, of which 6 were waited for; matrix products, arithmetic and copies ran while one was open for 35% of the time, Pallas kernels for 0%

profile of v1, /device:TPU:16, one launch (start us, length us, event | category | flops | bytes accessed | tf_op | source)
XLA Modules:
  0.0 187.9 jit_solution(13286867920029367560)
XLA Ops:
  7.2 1.9 %copy.48 = bf16[128,1024]{0,1:T(8,128)(2,1)} copy(bf16[128,1024]{1,0:T(8,128)(2,1)} %param.22) | data formatting | bytes 524288 | tf_op args[8]
  13.6 2.3 %add_convert_fusion = bf16[8,8,64,128]{3,2,1,0:T(8,128)(2,1)} fusion(bf16[128,8,8,64]{0,3,2,1:T(8,128)(2,1)S(1)} %bitcast.130, f32[128,8,8]{0,2,1:T(8,128)S(1)} %get-tuple-element.366, f32[8,8]{1,0:T(8,128)S(1)} %mul.195, bf16[128,8,128,1]{2,1,0,3:T(8,128)(2,1)S(1)} %bitcast.135), kind=kOutput, calls=%fused_computation.42 | convolution fusion | flops 807403520 | bytes 2392320 | tf_op jit(solution)/shard_map/while/body/eval_jaxpr/sgkp,sgn->gkpn/dot_general | solution.py:85
  16.1 11.4 %collective-permute-done = bf16[128,1024]{0,1:T(8,128)(2,1)S(1)} collective-permute-done((bf16[128,1024]{0,1:T(8,128)(2,1)S(1)}, bf16[128,1024]{0,1:T(8,128)(2,1)S(1)}, u32[]{:S(2)}, u32[]{:S(2)}) %collective-permute-start) | collective-permute-done | bytes 262176 | tf_op jit(solution)/shard_map/ppermute | solution.py:22
  27.9 8.3 %collective-permute-done.1 = bf16[128,1024]{0,1:T(8,128)(2,1)S(1)} collective-permute-done((bf16[128,1024]{0,1:T(8,128)(2,1)S(1)}, bf16[128,1024]{0,1:T(8,128)(2,1)S(1)}, u32[]{:S(2)}, u32[]{:S(2)}) %collective-permute-start.1) | collective-permute-done | bytes 262176 | tf_op jit(solution)/shard_map/ppermute | solution.py:22
  36.2 2.5 %collective-permute-start.2 = (bf16[128,1024]{0,1:T(8,128)(2,1)S(1)}, bf16[128,1024]{0,1:T(8,128)(2,1)S(1)}, u32[]{:S(2)}, u32[]{:S(2)}) collective-permute-start(bf16[128,1024]{0,1:T(8,128)(2,1)S(1)} %collective-permute-done.1), channel_id=1, source_target_pairs={{0,1},{1,2},{2,3},{3,4},{4,5},{5,6},{6,7},{7,0},{8,9},{9,10},{10,1... | collective-permute-start | bytes 786440 | tf_op jit(solution)/shard_map/ppermute | solution.py:22
  38.7 6.3 %collective-permute-done.2 = bf16[128,1024]{0,1:T(8,128)(2,1)S(1)} collective-permute-done((bf16[128,1024]{0,1:T(8,128)(2,1)S(1)}, bf16[128,1024]{0,1:T(8,128)(2,1)S(1)}, u32[]{:S(2)}, u32[]{:S(2)}) %collective-permute-start.2) | collective-permute-done | bytes 262176 | tf_op jit(solution)/shard_map/ppermute | solution.py:22
  45.3 5.6 %collective-permute-done.3 = bf16[128,1024]{0,1:T(8,128)(2,1)} collective-permute-done((bf16[128,1024]{0,1:T(8,128)(2,1)S(1)}, bf16[128,1024]{0,1:T(8,128)(2,1)}, u32[]{:S(2)}, u32[]{:S(2)}) %collective-permute-start.3) | collective-permute-done | bytes 262176 | tf_op jit(solution)/shard_map/ppermute | solution.py:22
  55.5 16.9 %all-reduce = bf16[512]{0:T(512)(128)(2,1)S(1)} all-reduce(bf16[512]{0:T(512)(128)(2,1)S(1)} %dynamic-update-slice), channel_id=2, replica_groups=mesh['dp'=4,'seq'=8] {'seq'}, use_global_device_ids=true, to_apply=%add | all-reduce | flops 512 | bytes 2048
  74.2 2.3 %copy.47 = bf16[128,4096]{0,1:T(8,128)(2,1)} copy(bf16[128,4096]{1,0:T(8,128)(2,1)} %param.15) | data formatting | bytes 2097152 | tf_op args[1]
  77.9 3.9 %fusion.18 = f32[8,8,128,64]{2,3,1,0:T(8,128)} fusion(bf16[128,8,8,64]{0,3,2,1:T(8,128)(2,1)} %bitcast.131, f32[8,8,128]{2,1,0:T(8,128)S(1)} %bitcast.134, f32[8,128,128]{2,1,0:T(8,128)S(1)} %fusion.36, pred[128,128]{1,0:T(8,128)(4,1)S(1)} %iota_compare_fusion), kind=kOutput, calls=%fused_computation.31 | convolution fusion | flops 138412032 | bytes 3719168 | tf_op jit(solution)/shard_map/while/body/eval_jaxpr/gkts,sgkp->tgkp/dot_general | solution.py:75
  81.8 13.1 %collective-permute-done.5 = bf16[128,1024]{0,1:T(8,128)(2,1)S(1)} collective-permute-done((bf16[128,1024]{0,1:T(8,128)(2,1)}, bf16[128,1024]{0,1:T(8,128)(2,1)S(1)}, u32[]{:S(2)}, u32[]{:S(2)}) %collective-permute-start.5) | collective-permute-done | bytes 262176 | tf_op jit(solution)/shard_map/ppermute | solution.py:22
  94.9 2.3 %fusion.34 = f32[8,8,64,128]{3,2,1,0:T(8,128)} fusion(bf16[128,8,128,1]{2,1,0,3:T(8,128)(2,1)S(1)} %bitcast.127), kind=kOutput, calls=%fused_computation.52 | convolution fusion | flops 805306368 | bytes 2359296 | tf_op jit(solution)/shard_map/while/body/eval_jaxpr/tgn,gkpn->tgkp/dot_general | solution.py:77
  97.2 16.3 %collective-permute-done.6 = bf16[128,1024]{0,1:T(8,128)(2,1)S(1)} collective-permute-done((bf16[128,1024]{0,1:T(8,128)(2,1)S(1)}, bf16[128,1024]{0,1:T(8,128)(2,1)S(1)}, u32[]{:S(2)}, u32[]{:S(2)}) %collective-permute-start.6) | collective-permute-done | bytes 262176 | tf_op jit(solution)/shard_map/ppermute | solution.py:22
  120.4 36.3 %while.38 = (s32[]{:T(128)}, f32[128,8,4]{0,2,1:T(4,128)S(1)}, f32[128,8,4]{0,2,1:T(4,128)S(1)}, f32[128,8,4,128]{0,3,2,1:T(8,128)}, bf16[1024,1024]{0,1:T(8,128...) while((s32[]{:T(128)}, f32[128,8,4]{0,2,1:T(4,128)S(1)}, ...), condition=%wide.region_7.8_spmd.clone, body=%wide.region_4.7_spmd.clone.sunk | while | flops 1102664320 | bytes 70784216 | solution.py:191
  120.4 2.6 %constant_dynamic-slice_fusion.4 = (bf16[512,1024]{0,1:T(8,128)(2,1)}, bf16[512,1024]{0,1:T(8,128)(2,1)S(1)}) fusion(bf16[1024,1024]{0,1:T(8,128)(2,1)} %get-tuple-element.512, s32[]{:T(128)S(6)} %select_n.111, bf16[1024,1024]{0,1:T(8,128)(2,1)} %get-tuple-element.510), kind=kLoop, calls=%fused_computation.20.clone.1 | loop fusion | bytes 4194308 | tf_op jit(solution)/shard_map/while/body/eval_jaxpr/dynamic_slice | solution.py:180
  123.2 4.7 %fusion.68 = (f32[128,8,4]{0,2,1:T(4,128)S(1)}, f32[8,512,128,4]{2,1,3,0:T(8,128)}) fusion(pred[128,512]{0,1:T(8,128)(4,1)S(1)} %broadcast_compare_fusion.2, bf16[512,8,128,1]{0,2,3,1:T(8,128)(2,1)S(1)} %bitcast.122, bf16[128,8,4,128]{3,0,2,1:T(8,128)(2,1)S(1)} %get-tuple-element.511), kind=kOutput, calls=%fused_computation.6.clone.1 | convolution fusion | flops 543158272 | bytes 10567680 | tf_op jit(solution)/shard_map/while/body/eval_jaxpr/qgkd,sgd->qgks/dot_general | solution.py:103
  127.9 4.7 %fusion.69 = f32[128,8,4]{0,2,1:T(4,128)S(1)} fusion(f32[8,512,128,4]{2,1,3,0:T(8,128)} %get-tuple-element.457, f32[128,8,4]{0,2,1:T(4,128)S(1)} %select_maximum_fusion.2, pred[128,512]{0,1:T(8,128)(4,1)S(1)} %broadcast_compare_fusion.2), kind=kLoop, calls=%fused_computation.8.clone.1 | loop fusion | flops 10481664 | bytes 8486912 | tf_op jit(solution)/shard_map/while/body/eval_jaxpr/reduce_sum | solution.py:112
  133.8 4.6 %bitcast_add_fusion.2 = f32[128,8,4,128]{0,3,2,1:T(8,128)} fusion(f32[128,8,4,128]{0,3,2,1:T(8,128)} %get-tuple-element.497, bf16[512,8,128,1]{0,2,3,1:T(8,128)(2,1)} %bitcast.124, f32[8,512,128,4]{2,1,3,0:T(8,128)S(1)} %copy-done, f32[128,8,4]{0,2,1:T(4,128)S(1)} %select_maximum_fusion.2, pred[128,512]{0,1:T(8,128)(4,1)S(1)} %broadcast_compare_fusion.2, ...), kind=kOutput, calls=%fused_computation.11.clone.1 | convolution fusion | flops 548929536 | bytes 13729793 | tf_op jit(solution)/shard_map/while/body/eval_jaxpr/qgks,sgd->qgkd/dot_general | solution.py:113
  138.4 2.6 %constant_dynamic-slice_fusion.4 = (bf16[512,1024]{0,1:T(8,128)(2,1)}, bf16[512,1024]{0,1:T(8,128)(2,1)S(1)}) fusion(bf16[1024,1024]{0,1:T(8,128)(2,1)} %get-tuple-element.512, s32[]{:T(128)S(6)} %select_n.111, bf16[1024,1024]{0,1:T(8,128)(2,1)} %get-tuple-element.510), kind=kLoop, calls=%fused_computation.20.clone.1 | loop fusion | bytes 4194308 | tf_op jit(solution)/shard_map/while/body/eval_jaxpr/dynamic_slice | solution.py:180
  141.2 4.7 %fusion.68 = (f32[128,8,4]{0,2,1:T(4,128)S(1)}, f32[8,512,128,4]{2,1,3,0:T(8,128)}) fusion(pred[128,512]{0,1:T(8,128)(4,1)S(1)} %broadcast_compare_fusion.2, bf16[512,8,128,1]{0,2,3,1:T(8,128)(2,1)S(1)} %bitcast.122, bf16[128,8,4,128]{3,0,2,1:T(8,128)(2,1)S(1)} %get-tuple-element.511), kind=kOutput, calls=%fused_computation.6.clone.1 | convolution fusion | flops 543158272 | bytes 10567680 | tf_op jit(solution)/shard_map/while/body/eval_jaxpr/qgkd,sgd->qgks/dot_general | solution.py:103
  146.0 4.7 %fusion.69 = f32[128,8,4]{0,2,1:T(4,128)S(1)} fusion(f32[8,512,128,4]{2,1,3,0:T(8,128)} %get-tuple-element.457, f32[128,8,4]{0,2,1:T(4,128)S(1)} %select_maximum_fusion.2, pred[128,512]{0,1:T(8,128)(4,1)S(1)} %broadcast_compare_fusion.2), kind=kLoop, calls=%fused_computation.8.clone.1 | loop fusion | flops 10481664 | bytes 8486912 | tf_op jit(solution)/shard_map/while/body/eval_jaxpr/reduce_sum | solution.py:112
  151.8 4.9 %bitcast_add_fusion.2 = f32[128,8,4,128]{0,3,2,1:T(8,128)} fusion(f32[128,8,4,128]{0,3,2,1:T(8,128)} %get-tuple-element.497, bf16[512,8,128,1]{0,2,3,1:T(8,128)(2,1)} %bitcast.124, f32[8,512,128,4]{2,1,3,0:T(8,128)S(1)} %copy-done, f32[128,8,4]{0,2,1:T(4,128)S(1)} %select_maximum_fusion.2, pred[128,512]{0,1:T(8,128)(4,1)S(1)} %broadcast_compare_fusion.2, ...), kind=kOutput, calls=%fused_computation.11.clone.1 | convolution fusion | flops 548929536 | bytes 13729793 | tf_op jit(solution)/shard_map/while/body/eval_jaxpr/qgks,sgd->qgkd/dot_general | solution.py:113
  156.7 1.8 divide_convert_fusion
  159.9 14.5 %while.37 = (s32[]{:T(128)}, f32[64,64,128]{2,1,0:T(8,128)S(1)}, s32[]{:T(128)}, bf16[8,64]{1,0:T(8,128)(2,1)S(1)}, bf16[8,64,64,128]{3,2,1,0:T(8,128)(2,1)}, /*index=5*/s32[]{:T(128)}, s32[]{:T(128)}) while((s32[]{:T(128)}, f32[64,64,128]{2,1,0:T(8,128)S(1)}, s32[]{:T(128)}, bf16[8,64]{1,0:T(8,128)(2,1)S(1)}, ...), condition=%wide.region_2.3_spmd.clone, body=%wide.region_1.2_spmd.clone.sunk | while | flops 2621508 | bytes 5243625 | solution.py:53
  159.9 1.9 fusion.63
  161.8 1.8 fusion.63
  163.6 1.8 fusion.63
  165.4 1.8 fusion.63
  167.2 1.8 fusion.63
  169.1 1.8 fusion.63
  170.9 1.8 fusion.63
  174.5 4.3 %multiply_reduce_fusion = (f32[128,8,8]{0,2,1:T(8,128)S(1)}, f32[128,8,8,64]{0,3,2,1:T(8,128)S(1)}) fusion(bf16[128,4096]{0,1:T(8,128)(2,1)S(1)} %copy-done.1, f32[8,8,64,128]{3,2,1,0:T(8,128)S(1)} %bitcast.123, bf16[128,8,128,1]{2,1,0,3:T(8,128)(2,1)S(1)} %bitcast.128, f32[128,8,8]{0,2,1:T(8,128)S(1)} %get-tuple-element.365, ...), kind=kOutput, calls=%fused_computation.41 | convolution fusion | flops 811589632 | bytes 9764864 | tf_op jit(solution)/shard_map/tgn,gkpn->tgkp/dot_general | solution.py:200
  (109 shorter events, 27.1 us)
Async XLA Ops:
  7.2 8.7 %copy-start.12 = (bf16[128,1024]{1,0:T(8,128)(2,1)S(1)}, bf16[128,1024]{1,0:T(8,128)(2,1)}, u32[]{:S(2)}) copy-start(bf16[128,1024]{1,0:T(8,128)(2,1)} %param.23) | copy-start | bytes 786436
  7.2 43.9 %copy-start.4 = (bf16[128,4096]{1,0:T(8,128)(2,1)S(1)}, bf16[128,4096]{1,0:T(8,128)(2,1)}, u32[]{:S(2)}) copy-start(bf16[128,4096]{1,0:T(8,128)(2,1)} %param.21) | copy-start | bytes 3145732
  7.2 113.2 %all-gather.6.cloned.1.call-start = ((), (), s32[]{:S(2)}) async-start(), calls=%async_computation.1 | async-start | bytes 2359296 | tf_op jit(solution)/shard_map/all_gather | solution.py:173
  9.2 150.7 %all-gather.4.cloned.1.call-start = ((), (), s32[]{:S(2)}) async-start(), calls=%async_computation | async-start | bytes 9437184 | tf_op jit(solution)/shard_map/all_gather | solution.py:36
  12.3 38.7 %copy-start.5 = (bf16[128,4096]{0,1:T(8,128)(2,1)}, bf16[128,4096]{0,1:T(8,128)(2,1)S(1)}, u32[]{:S(2)}) copy-start(bf16[128,4096]{0,1:T(8,128)(2,1)S(1)} %copy.43) | copy-start | bytes 3145732
  13.5 40.5 %copy-start.14 = (u32[32]{0:T(128)S(1)}, u32[32]{0:T(128)}, u32[]{:S(2)}) copy-start(u32[32]{0:T(128)} %constant.143) | copy-start | bytes 388
  16.0 11.5 %collective-permute-start = (bf16[128,1024]{0,1:T(8,128)(2,1)S(1)}, bf16[128,1024]{0,1:T(8,128)(2,1)S(1)}, u32[]{:S(2)}, u32[]{:S(2)}) collective-permute-start(bf16[128,1024]{0,1:T(8,128)(2,1)S(1)} %copy.50), channel_id=1, source_target_pairs={{0,1},{1,2},{2,3},{3,4},{4,5},{5,6},{6,7},{7,0},{8,9},{9,10},{10,1... | collective-permute-start | bytes 786440 | tf_op jit(solution)/shard_map/ppermute | solution.py:22
  27.5 23.5 %copy-start.6 = (bf16[128,1024]{0,1:T(8,128)(2,1)}, bf16[128,1024]{0,1:T(8,128)(2,1)S(1)}, u32[]{:S(2)}) copy-start(bf16[128,1024]{0,1:T(8,128)(2,1)S(1)} %collective-permute-done) | copy-start | bytes 786436
  27.5 8.7 %collective-permute-start.1 = (bf16[128,1024]{0,1:T(8,128)(2,1)S(1)}, bf16[128,1024]{0,1:T(8,128)(2,1)S(1)}, u32[]{:S(2)}, u32[]{:S(2)}) collective-permute-start(bf16[128,1024]{0,1:T(8,128)(2,1)S(1)} %collective-permute-done), channel_id=1, source_target_pairs={{0,1},{1,2},{2,3},{3,4},{4,5},{5,6},{6,7},{7,0},{8,9},{9,10},{10,1... | collective-permute-start | bytes 786440 | tf_op jit(solution)/shard_map/ppermute | solution.py:22
  36.2 14.8 %copy-start.8 = (bf16[128,1024]{0,1:T(8,128)(2,1)}, bf16[128,1024]{0,1:T(8,128)(2,1)S(1)}, u32[]{:S(2)}) copy-start(bf16[128,1024]{0,1:T(8,128)(2,1)S(1)} %collective-permute-done.1) | copy-start | bytes 786436
  36.2 8.8 %collective-permute-start.2 = (bf16[128,1024]{0,1:T(8,128)(2,1)S(1)}, bf16[128,1024]{0,1:T(8,128)(2,1)S(1)}, u32[]{:S(2)}, u32[]{:S(2)}) collective-permute-start(bf16[128,1024]{0,1:T(8,128)(2,1)S(1)} %collective-permute-done.1), channel_id=1, source_target_pairs={{0,1},{1,2},{2,3},{3,4},{4,5},{5,6},{6,7},{7,0},{8,9},{9,10},{10,1... | collective-permute-start | bytes 786440 | tf_op jit(solution)/shard_map/ppermute | solution.py:22
  45.0 6.0 %copy-start.10 = (bf16[128,1024]{0,1:T(8,128)(2,1)}, bf16[128,1024]{0,1:T(8,128)(2,1)S(1)}, u32[]{:S(2)}) copy-start(bf16[128,1024]{0,1:T(8,128)(2,1)S(1)} %collective-permute-done.2) | copy-start | bytes 786436
  45.0 5.9 %collective-permute-start.3 = (bf16[128,1024]{0,1:T(8,128)(2,1)S(1)}, bf16[128,1024]{0,1:T(8,128)(2,1)}, u32[]{:S(2)}, u32[]{:S(2)}) collective-permute-start(bf16[128,1024]{0,1:T(8,128)(2,1)S(1)} %collective-permute-done.2), channel_id=1, source_target_pairs={{0,1},{1,2},{2,3},{3,4},{4,5},{5,6},{6,7},{7,0},{8,9},{9,10},{10,1... | collective-permute-start | bytes 786440 | tf_op jit(solution)/shard_map/ppermute | solution.py:22
  50.9 26.9 %collective-permute-start.4 = (bf16[128,1024]{0,1:T(8,128)(2,1)}, bf16[128,1024]{0,1:T(8,128)(2,1)}, u32[]{:S(2)}, u32[]{:S(2)}) collective-permute-start(bf16[128,1024]{0,1:T(8,128)(2,1)} %collective-permute-done.3), channel_id=1, source_target_pairs={{0,1},{1,2},{2,3},{3,4},{4,5},{5,6},{6,7},{7,0},{8,9},{9,10},{10,1... | collective-permute-start | bytes 786440 | tf_op jit(solution)/shard_map/ppermute | solution.py:22
  76.4 18.4 %copy-start.2 = (bf16[16,8,8,128]{3,2,1,0:T(8,128)(2,1)S(1)}, bf16[16,8,8,128]{3,2,1,0:T(8,128)(2,1)}, u32[]{:S(2)}) copy-start(bf16[16,8,8,128]{3,2,1,0:T(8,128)(2,1)} %copy.73) | copy-start | bytes 786436
  77.8 17.1 %collective-permute-start.5 = (bf16[128,1024]{0,1:T(8,128)(2,1)}, bf16[128,1024]{0,1:T(8,128)(2,1)S(1)}, u32[]{:S(2)}, u32[]{:S(2)}) collective-permute-start(bf16[128,1024]{0,1:T(8,128)(2,1)} %collective-permute-done.4), channel_id=1, source_target_pairs={{0,1},{1,2},{2,3},{3,4},{4,5},{5,6},{6,7},{7,0},{8,9},{9,10},{10,1... | collective-permute-start | bytes 786440 | tf_op jit(solution)/shard_map/ppermute | solution.py:22
  77.9 37.9 %copy-start.11 = (bf16[128,1024]{0,1:T(8,128)(2,1)S(1)}, bf16[128,1024]{0,1:T(8,128)(2,1)}, u32[]{:S(2)}) copy-start(bf16[128,1024]{0,1:T(8,128)(2,1)} %copy-done.10) | copy-start | bytes 786436
  81.8 34.1 %copy-start.9 = (bf16[128,1024]{0,1:T(8,128)(2,1)S(1)}, bf16[128,1024]{0,1:T(8,128)(2,1)}, u32[]{:S(2)}) copy-start(bf16[128,1024]{0,1:T(8,128)(2,1)} %copy-done.8) | copy-start | bytes 786436
  81.8 34.2 %copy-start.7 = (bf16[128,1024]{0,1:T(8,128)(2,1)S(1)}, bf16[128,1024]{0,1:T(8,128)(2,1)}, u32[]{:S(2)}) copy-start(bf16[128,1024]{0,1:T(8,128)(2,1)} %copy-done.6) | copy-start | bytes 786436
  94.9 18.6 %collective-permute-start.6 = (bf16[128,1024]{0,1:T(8,128)(2,1)S(1)}, bf16[128,1024]{0,1:T(8,128)(2,1)S(1)}, u32[]{:S(2)}, u32[]{:S(2)}) collective-permute-start(bf16[128,1024]{0,1:T(8,128)(2,1)S(1)} %collective-permute-done.5), channel_id=1, source_target_pairs={{0,1},{1,2},{2,3},{3,4},{4,5},{5,6},{6,7},{7,0},{8,9},{9,10},{10,1... | collective-permute-start | bytes 786440 | tf_op jit(solution)/shard_map/ppermute | solution.py:22
  127.9 5.9 %copy-start = (f32[8,512,128,4]{2,1,3,0:T(8,128)S(1)}, f32[8,512,128,4]{2,1,3,0:T(8,128)}, u32[]{:S(2)}) copy-start(f32[8,512,128,4]{2,1,3,0:T(8,128)} %get-tuple-element.457) | copy-start | bytes 25165828 | tf_op jit(solution)/shard_map/while
  146.0 5.8 %copy-start = (f32[8,512,128,4]{2,1,3,0:T(8,128)S(1)}, f32[8,512,128,4]{2,1,3,0:T(8,128)}, u32[]{:S(2)}) copy-start(f32[8,512,128,4]{2,1,3,0:T(8,128)} %get-tuple-element.457) | copy-start | bytes 25165828 | tf_op jit(solution)/shard_map/while
  159.9 14.5 %copy-start.1 = (bf16[128,4096]{0,1:T(8,128)(2,1)S(1)}, bf16[128,4096]{0,1:T(8,128)(2,1)}, u32[]{:S(2)}) copy-start(bf16[128,4096]{0,1:T(8,128)(2,1)} %copy.47) | copy-start | bytes 3145732
  159.9 14.6 %copy-start.3 = (bf16[16,8,8,128]{3,2,1,0:T(8,128)(2,1)S(1)}, bf16[16,8,8,128]{3,2,1,0:T(8,128)(2,1)}, u32[]{:S(2)}) copy-start(bf16[16,8,8,128]{3,2,1,0:T(8,128)(2,1)} %copy.73) | copy-start | bytes 786436
  174.5 4.3 %copy-start.13 = (f32[4096]{0:T(1024)S(1)}, f32[4096]{0:T(1024)}, u32[]{:S(2)}) copy-start(f32[4096]{0:T(1024)} %param.20) | copy-start | bytes 49156
Sparse Core Ops, SparseCore 0:
  9.6 35.7 all-gather.5
  47.0 87.1 all-gather.3
